TPU v7x, 32 devices: a whole 2x2x4 slice. The times are simulated.
32 devices in a mesh: patch: 8 (over y, x, core), grp: 4 (over z).
Axes of the slice: x: 2, y: 2, z: 4, core: 2. Of those that a mesh axis runs over, the one named last changes fastest.
Arguments:
- cells: int32 [3, 8, 4, 32, 128], P(None, 'patch', 'grp'), may hold values from 0 to 15, as said below
- offsets: float32 [3, 8, 4, 32, 128], P(None, 'patch', 'grp'), may hold values from -0.5 to 0.5
- charges: float32 [8, 4, 32, 128], P('patch', 'grp'), may hold values from -4 to 4
- masses: float32 [8, 4, 32, 128], P('patch', 'grp'), may hold values from 1 to 16
- velocity: float32 [3, 8, 4, 32, 128], P(None, 'patch', 'grp'), may hold values from -5 to 5
- task_first: int32 [8, 4, 32], P('patch', 'grp'), may hold values from 0 to 127, as said below
- task_second: int32 [8, 4, 32], P('patch', 'grp'), may hold values from 0 to 255, as said below
- task_count: int32 [8, 4], P('patch', 'grp'), may hold values from 0 to 32, as said below
- kernel_taps: float32 [6, 17], replicated, may hold values from -3 to 3
Outputs:
- displacement: float32 [3, 8, 4, 32, 128], P(None, 'patch', 'grp')
- velocities: float32 [3, 8, 4, 32, 128], P(None, 'patch', 'grp')
Inputs may be any that keep to these rules, and one draw needn't show every extreme that they name: `cells`: components x, y, z lie below 8, 16, 8. `task_first`: A patch of the host's slab, written strip * 32 + place. `task_second`: slab step * 4 * 32 + strip * 32 + place of one of the 13 forward neighbours of the first patch, periodic: in the next slab any of the 9 with strip and place within one; in the same slab strip + 0 with place + 1, or strip + 1 with place within one. A pair may repeat. `task_count`: on each slab the 4 counts add up to exactly 64; every slab has one device with 32 live slots and one with none. Slots at or past the count are ignored.
All inputs are finite; a program needn't handle non-finite values.
Results may differ from a plain program's by a relative error of at most 0.000068.
Values sent between devices are 32-bit elements; how exact they have to be, the bound alone decides.
No kernel may reach another device: no remote copies, remote signals or barrier semaphores. Data moves between devices by JAX's collectives and lax.ppermute only.
A program may use at most 64 MiB of HBM per device.

v0:
```python
import functools

import jax
import jax.numpy as jnp
from jax import lax
from jax.experimental import pallas as pl
from jax.experimental.pallas import tpu as pltpu
from jax.sharding import PartitionSpec as P

MXD = 8
MYD = 16
PZ = 8
RADIUS = 8

time_step = 0.5
reach_sq = 64.0
soft_end = 65.0
push_scale = 1.0 / 4096.0

XO = MXD + 2
YO = MYD + 2
YR = 24
XW = XO + 2 * RADIUS
YE = RADIUS + 2
NE = 104
NS = 184
N2 = 40

f32 = jnp.float32
bf16 = jnp.bfloat16
i32 = jnp.int32


def split(x):
    hi = x.astype(bf16)
    lo = (x - hi.astype(f32)).astype(bf16)
    return hi, lo


def dot(a, b, dims=(((1,), (0,)), ((), ()))):
    return lax.dot_general(a, b, dims, preferred_element_type=f32)


def dot3(a, b, dims=(((1,), (0,)), ((), ()))):
    ah, al = a
    bh, bl = b
    return dot(ah, bh, dims) + (dot(al, bh, dims) + dot(ah, bl, dims))


NT = (((1,), (1,)), ((), ()))
TN = (((0,), (0,)), ((), ()))


def iota(shape, dim):
    return lax.broadcasted_iota(i32, shape, dim)


def spline(frac):
    weights = (0.5 * (0.5 - frac) ** 2, 0.75 - frac * frac, 0.5 * (0.5 + frac) ** 2)
    slopes = (frac - 0.5, -2.0 * frac, 0.5 + frac)
    return weights, slopes


def place3(rows, base, values):
    out = jnp.where(rows == base, values[0], 0.0)
    out = jnp.where(rows == base + 1, values[1], out)
    return jnp.where(rows == base + 2, values[2], out)


def pair_rows(ref, c, m):
    if c is None:
        return jnp.concatenate([ref[2 * m : 2 * m + 1, :], ref[2 * m + 1 : 2 * m + 2, :]], axis=1)
    return jnp.concatenate([ref[c, 2 * m : 2 * m + 1, :], ref[c, 2 * m + 1 : 2 * m + 2, :]], axis=1)


def pair_base_z(cz, atoms):
    second = (iota(cz.shape, 1) >= atoms).astype(i32)
    return cz + (PZ - 1) + PZ * second


def spread_kernel(cells, frac, charge, first, second, count, own, pk_lo, pk_hi, pos, lists, acc):
    places, atoms = charge.shape
    depth = places * PZ
    for c in range(3):
        start = cells[c].astype(f32) + frac[c]
        for dst, at in ((pos, 0), (pk_lo, 2 * NE), (pk_hi, 2 * NE)):
            dst[at + c * places : at + (c + 1) * places, :] = start
    q = charge[...]
    for dst, at in ((pos, 0), (pk_lo, 2 * NE), (pk_hi, 2 * NE)):
        dst[at + 3 * places : at + 4 * places, :] = q
    slots = first.shape[1]
    zero = jnp.zeros((1, atoms - slots), f32)
    block = jnp.concatenate(
        [
            jnp.concatenate([first[...].astype(f32), zero], axis=1),
            jnp.concatenate([second[...].astype(f32), zero], axis=1),
            jnp.broadcast_to(count[...].astype(f32), (1, atoms)),
            jnp.zeros((5, atoms), f32),
        ],
        axis=0,
    )
    at = 2 * NE + 4 * places
    lists[...] = block
    pk_lo[at : at + 8, :] = block
    pk_hi[at : at + 8, :] = block
    acc[...] = jnp.zeros_like(acc)
    y_rows = iota((YR, 2 * atoms), 0)
    x_rows = iota((16, 2 * atoms), 0)
    z_rows = iota((4 * PZ, 2 * atoms), 0)
    for m in range(places // 2):
        wx = place3(x_rows, pair_rows(cells, 0, m), spline(pair_rows(frac, 0, m))[0])
        wy = place3(y_rows, pair_rows(cells, 1, m), spline(pair_rows(frac, 1, m))[0])
        wz = place3(
            z_rows, pair_base_z(pair_rows(cells, 2, m), atoms), spline(pair_rows(frac, 2, m))[0]
        )
        wy = wy * pair_rows(charge, None, m)
        table = jnp.concatenate([wx[x : x + 1, :] * wy for x in range(XO)], axis=0)
        rows = pl.ds(2 * PZ * m, 4 * PZ)
        acc[rows, : XO * YR] += dot3(split(wz), split(table), NT)
    acc[depth : depth + PZ, :] += acc[0:PZ, :]
    acc[PZ : 2 * PZ, :] += acc[depth + PZ : depth + 2 * PZ, :]
    grid = jnp.transpose(acc[PZ : PZ + depth, :])
    own[...] = grid[: XO * YR, :]
    pk_lo[0 : 2 * NE, :] = jnp.zeros((2 * NE, 128), f32)
    pk_hi[0 : 2 * NE, :] = jnp.zeros((2 * NE, 128), f32)
    for x in range(XO):
        for half in range(2):
            dst = pl.ds(half * NE + x * YE, YE)
            lanes = slice(half * 128, half * 128 + 128)
            pk_lo[dst, :] = own[x * YR : x * YR + YE, lanes]
            pk_hi[dst, :] = own[x * YR + YO - YE : x * YR + YO, lanes]


def add_side(force, posr, cols, blk, r, p, places, offsets):
    off_x, off_y, off_z = offsets
    shape = (8, 128)
    xr = jnp.broadcast_to(posr[pl.ds(r, 1), :] + off_x, shape)
    yr = jnp.broadcast_to(posr[pl.ds(places + r, 1), :] + off_y, shape)
    zr = jnp.broadcast_to(posr[pl.ds(2 * places + r, 1), :] + off_z, shape)
    ax = jnp.zeros(shape, f32)
    ay = jnp.zeros(shape, f32)
    az = jnp.zeros(shape, f32)
    ix = jnp.full(shape, p, i32)
    iy, iz, iq = ix + places, ix + 2 * places, ix + 3 * places
    for k in range(16):
        col = cols[blk, 8 * k : 8 * k + 8, :]
        dx = xr - jnp.take_along_axis(col, ix, axis=1)
        dy = yr - jnp.take_along_axis(col, iy, axis=1)
        dz = zr - jnp.take_along_axis(col, iz, axis=1)
        qs = jnp.take_along_axis(col, iq, axis=1)
        soft = (dx * dx + dy * dy) + (dz * dz + 1.0)
        reach = jnp.maximum(soft_end - soft, 0.0)
        rs = lax.rsqrt(soft)
        t = reach * rs
        c = (t * t) * (rs * qs)
        ax = ax + c * dx
        ay = ay + c * dy
        az = az + c * dz
    for c, a in enumerate((ax, ay, az)):
        rows = pl.ds(pl.multiple_of((c * places + r) * 8, 8), 8)
        force[rows, :] += a


def folded_force(force, posr, places, c):
    part = force[c * places * 8 : (c + 1) * places * 8, :]
    total = jnp.sum(part.reshape(places, 8, 128), axis=1)
    return total * (posr[3 * places : 4 * places, :] * push_scale)


def add_self(force, posr, cols, places):
    def body(r, carry):
        add_side(force, posr, cols, 0, r, r, places, (0.0, 0.0, 0.0))
        return carry

    lax.fori_loop(0, places, body, 0)


def add_listed(force, posr, cols, work, places, slot_of):
    bits = places.bit_length() - 1

    def body(n, carry):
        code = work[n + 1]
        r = code & (places - 1)
        p = (code >> bits) & (places - 1)
        blk = code >> (2 * bits)
        dslab = blk // 3 - 1
        dstrip = blk % 3 - 1
        dz = ((r - p + 1) & (places - 1)) - 1
        off = (
            (-MXD * dslab).astype(f32),
            (-MYD * dstrip).astype(f32),
            (PZ * dz).astype(f32),
        )
        add_side(force, posr, cols, slot_of(blk), r, p, places, off)
        return carry

    lax.fori_loop(0, work[0], body, 0)


def wrap_step(delta, count):
    return jnp.where(delta > 1, delta - count, jnp.where(delta < -1, delta + count, delta))


def list_tasks(lists, number, below, work_near, work_far, places, strips):
    bits = places.bit_length() - 1
    per_slab = places * strips
    mine = lax.axis_index("grp")

    def code(r, dslab, strip, p):
        blk = (dslab + 1) * 3 + wrap_step(strip - mine, strips) + 1
        blk = jnp.clip(blk, 0, 8)
        return r + places * (p + places * blk)

    def each_list(h, carry):
        live = lists[h, 2, 0].astype(i32)

        def each(k, carry):
            near, far = carry
            a = lists[h, 0, k].astype(i32)
            b = lists[h, 1, k].astype(i32)
            upper = (b >= per_slab).astype(i32)
            rest = b - upper * per_slab
            a_strip, a_place = a >> bits, a & (places - 1)
            b_strip, b_place = rest >> bits, rest & (places - 1)
            if below:
                work_far[far + 1] = code(b_place, -1, a_strip, a_place)
                return near, far + upper * (b_strip == mine).astype(i32)
            left = (a_strip == mine).astype(i32)
            work_far[far + 1] = code(a_place, 1, b_strip, b_place)
            far = far + upper * left
            work_near[near + 1] = code(a_place, 0, b_strip, b_place)
            near = near + (1 - upper) * left
            work_near[near + 1] = code(b_place, 0, a_strip, a_place)
            near = near + (1 - upper) * (b_strip == mine).astype(i32)
            return near, far

        return lax.fori_loop(0, live, each, carry)

    near, far = lax.fori_loop(0, number, each_list, (jnp.int32(0), jnp.int32(0)))
    work_far[0] = far
    if not below:
        work_near[0] = near


def tap_lookup(taps, t, index):
    span = 2 * RADIUS + 1
    index = jnp.where((index >= 0) & (index < span), index, 127)
    row = jnp.broadcast_to(taps[t : t + 1, :], (8, 128))
    blocks = []
    for i in range(0, index.shape[0], 8):
        blocks.append(
            jnp.concatenate(
                [
                    jnp.take_along_axis(row, index[i : i + 8, j : j + 128], axis=1)
                    for j in range(0, index.shape[1], 128)
                ],
                axis=1,
            )
        )
    return jnp.concatenate(blocks, axis=0)


def line_table(taps, t, depth):
    half = depth // 2
    rows, lanes = iota((half, half), 0), iota((half, half), 1)
    same = tap_lookup(taps, t, lanes - rows + RADIUS)
    other = tap_lookup(taps, t, (lanes - rows + half + RADIUS) % depth)
    return jnp.concatenate(
        [jnp.concatenate([same, other], axis=1), jnp.concatenate([other, same], axis=1)], axis=0
    )


def plane_table(taps, t, x_of, y_of):
    lanes = x_of.shape[1]
    x_rows = iota((32, lanes), 0) - (RADIUS + 1)
    y_rows = iota((YR, lanes), 0) - 1
    along_x = tap_lookup(taps, t, x_rows - x_of + RADIUS)
    along_y = tap_lookup(taps, t, y_rows - y_of + RADIUS)
    return jnp.concatenate([along_x[x : x + 1, :] * along_y for x in range(XW)], axis=0)


def put_split(pair, rows, lanes, value):
    hi, lo = split(value)
    pair[0, rows, lanes] = hi
    pair[1, rows, lanes] = lo


def tables_kernel(
    taps_in, own, pos, line, edge_table, partial, force_out, taps, table, smooth, cols, force
):
    places = pos.shape[0] // 4
    depth = places * PZ
    terms = taps_in.shape[0]
    taps[...] = jnp.zeros_like(taps)
    taps[0:terms, 0 : taps_in.shape[1]] = taps_in[...]
    lane_own = iota((8, 256), 1)
    own_x = lane_own[0:1] // YR - 1
    own_y = lane_own[0:1] % YR - 1
    own_x = jnp.where(lane_own[0:1] < XO * YR, own_x, 1000)
    lane = iota((1, 256), 1)
    in_up = lane < XO * YE
    in_down = (lane >= NE) & (lane < NE + XO * YE)
    local = jnp.where(in_up, lane, lane - NE)
    edge_x = jnp.where(in_up | in_down, local // YE - 1, 1000)
    edge_y = local % YE + jnp.where(in_up, MYD - 1, -(RADIUS + 1))
    own_pair = split(jnp.concatenate([own[...], jnp.zeros((16, depth), f32)], axis=0))
    for t in range(terms):
        kz = line_table(taps, t, depth)
        kh, kl = split(kz)
        line[0, t] = kh
        line[1, t] = kl
        q = dot3(own_pair, (kh, kl))
        put_split(smooth, slice(t * 256, t * 256 + 256), slice(None), q)
        put_split(table, slice(None), slice(t * 256, t * 256 + 256), plane_table(taps, t, own_x, own_y))
        put_split(
            edge_table, slice(None), slice(t * 256, t * 256 + 256), plane_table(taps, t, edge_x, edge_y)
        )
    partial[...] = dot3((table[0], table[1]), (smooth[0], smooth[1]))
    cols[0] = jnp.transpose(pos[...])
    force[...] = jnp.zeros_like(force)
    add_self(force, pos, cols, places)
    force_out[...] = force[...]


def planes_kernel(
    *refs, number_far
):
    up, down, pos, lists = refs[:4]
    far = refs[4 : 4 + number_far]
    line, edge_table, partial = refs[4 + number_far : 7 + number_far]
    pk_lo, pk_hi, e_lo, e_hi, mid, smooth = refs[7 + number_far :]
    places = pos.shape[0] // 4
    terms = line.shape[1]
    block = jnp.concatenate(
        [
            jnp.concatenate([src[0:NE, :], src[NE : 2 * NE, :]], axis=1) for src in (up, down)
        ]
        + [jnp.zeros((256 - 2 * NE, 256), f32)],
        axis=0,
    )
    pair = split(block)
    for t in range(terms):
        q = dot3(pair, (line[0, t], line[1, t]))
        put_split(smooth, slice(t * 256, t * 256 + 256), slice(None), q)
    total = partial[...] + dot3((edge_table[0], edge_table[1]), (smooth[0], smooth[1]))
    mid[...] = total[RADIUS * YR : (RADIUS + XO) * YR, :]
    low = total[: XO * YR, :]
    high = total[2 * RADIUS * YR :, :]
    for half in range(2):
        lanes = slice(half * 128, half * 128 + 128)
        for x in range(XO):
            rows = pl.ds(half * NS + x * YO, YO)
            pk_lo[rows, :] = low[x * YR : x * YR + YO, lanes]
            pk_hi[rows, :] = high[x * YR : x * YR + YO, lanes]
        for x in range(2):
            rows = pl.ds(half * N2 + x * YO, YO)
            e_lo[rows, :] = low[x * YR : x * YR + YO, lanes]
            e_hi[rows, :] = high[(XO - 2 + x) * YR : (XO - 2 + x) * YR + YO, lanes]
        for dst, size, pad in ((pk_lo, NS, NS - XO * YO), (pk_hi, NS, NS - XO * YO), (e_lo, N2, N2 - 2 * YO), (e_hi, N2, N2 - 2 * YO)):
            dst[(half + 1) * size - pad : (half + 1) * size, :] = jnp.zeros((pad, 128), f32)
    rows = 4 * places
    for dst in (pk_lo, pk_hi):
        at = 2 * NS
        for src, begin in ((down, 2 * NE), (pos, 0), (up, 2 * NE)):
            dst[at : at + rows, :] = src[begin : begin + rows, :]
            at += rows
        for src, begin in [(lists, 0), (down, 2 * NE + rows), (up, 2 * NE + rows)] + [(r, 0) for r in far]:
            dst[at : at + 8, :] = src[begin : begin + 8, :]
            at += 8


def near_kernel(*refs, number_far, strips):
    up, down, pos, lists = refs[:4]
    far = refs[4 : 4 + number_far]
    force_in = refs[4 + number_far]
    force_out, work_near, work_far, held, cols, sem = refs[5 + number_far :]
    places = pos.shape[0] // 4
    rows = 4 * places
    sources = [lists.at[0:8], down.at[pl.ds(2 * NE + rows, 8)], up.at[pl.ds(2 * NE + rows, 8)]]
    sources += [r.at[0:8] for r in far]
    copies = [
        pltpu.make_async_copy(src, held.at[n], sem.at[n]) for n, src in enumerate(sources)
    ]
    for copy in copies:
        copy.start()
    force_out[...] = force_in[...]
    cols[0] = jnp.transpose(down[2 * NE : 2 * NE + rows, :])
    cols[1] = jnp.transpose(pos[...])
    cols[2] = jnp.transpose(up[2 * NE : 2 * NE + rows, :])
    for copy in copies:
        copy.wait()
    list_tasks(held, len(sources), False, work_near, work_far, places, strips)
    add_listed(force_out, pos, cols, work_near, places, lambda blk: blk - 3)


def sample_kernel(
    cells, frac, charge, masses, velocity, pos, mid, low, high, e_lo, e_hi, force_in, work_far,
    half_out, moved, work_below, force, held, cols, grid, turned, long, sem, *, strips
):
    places, atoms = charge.shape
    depth = places * PZ
    rows = 4 * places
    at = 2 * NS + 3 * rows
    copies = [
        pltpu.make_async_copy(low.at[pl.ds(at + 8 * n, 8)], held.at[n], sem.at[n]) for n in range(strips)
    ]
    for copy in copies:
        copy.start()
    grid[...] = jnp.zeros_like(grid)
    for x in range(XO):
        for half in range(2):
            lanes = slice(half * 128, half * 128 + 128)
            src = pl.ds(half * NS + x * YO, YO)
            value = mid[x * YR : x * YR + YO, lanes] + low[src, :] + high[src, :]
            if x < 2:
                value = value + e_lo[pl.ds(half * N2 + x * YO, YO), :]
            if x >= XO - 2:
                value = value + e_hi[pl.ds(half * N2 + (x - XO + 2) * YO, YO), :]
            grid[x * YR : x * YR + YO, lanes] = value
    body = jnp.transpose(grid[...])
    turned[PZ : PZ + depth, :] = body
    turned[0:PZ, :] = body[depth - PZ :, :]
    turned[PZ + depth : 2 * PZ + depth, :] = body[0:PZ, :]
    y_rows = iota((YR, 2 * atoms), 0)
    x_rows = iota((16, 2 * atoms), 0)
    z_rows = iota((4 * PZ, 2 * atoms), 0)
    for m in range(places // 2):
        vx, dx = spline(pair_rows(frac, 0, m))
        vy, dy = spline(pair_rows(frac, 1, m))
        vz, dz = spline(pair_rows(frac, 2, m))
        bx, by = pair_rows(cells, 0, m), pair_rows(cells, 1, m)
        bz = pair_base_z(pair_rows(cells, 2, m), atoms)
        wx, sx = place3(x_rows, bx, vx), place3(x_rows, bx, dx)
        wy, sy = place3(y_rows, by, vy), place3(y_rows, by, dy)
        both = jnp.concatenate([place3(z_rows, bz, vz), place3(z_rows, bz, dz)], axis=1)
        bh, bl = split(both)
        th, tl = split(turned[2 * PZ * m : 2 * PZ * m + 4 * PZ, :])
        sampled = dot(
            jnp.concatenate([th, th, tl], axis=0), jnp.concatenate([bh, bl, bh], axis=0), TN
        )
        shape = (YR, 2 * atoms)
        gx, gy, gz = jnp.zeros(shape, f32), jnp.zeros(shape, f32), jnp.zeros(shape, f32)
        for x in range(XO):
            plain = sampled[x * YR : (x + 1) * YR, : 2 * atoms]
            sloped = sampled[x * YR : (x + 1) * YR, 2 * atoms :]
            gx = gx + sx[x : x + 1, :] * plain
            gy = gy + wx[x : x + 1, :] * plain
            gz = gz + wx[x : x + 1, :] * sloped
        for c, value in enumerate((gx * wy, gy * sy, gz * wy)):
            line = jnp.sum(value, axis=0, keepdims=True)
            long[c, 2 * m : 2 * m + 1, :] = line[:, :atoms]
            long[c, 2 * m + 1 : 2 * m + 2, :] = line[:, atoms:]
    for n, src in enumerate((low, high)):
        for k in range(3):
            begin = 2 * NS + k * rows
            cols[3 * n + k] = jnp.transpose(src[begin : begin + rows, :])
    force[...] = force_in[...]
    add_listed(force, pos, cols, work_far, places, lambda blk: blk - 3)
    for copy in copies:
        copy.wait()
    list_tasks(held, strips, True, None, work_below, places, strips)
    add_listed(force, pos, cols, work_below, places, lambda blk: blk)
    inverse = time_step * (1.0 / masses[...])
    q = charge[...]
    for c in range(3):
        total = folded_force(force, pos, places, c) - 2.0 * q * long[c]
        half = velocity[c] + inverse * total
        half_out[c] = half
        moved[c * places : (c + 1) * places, :] = (
            pos[c * places : (c + 1) * places, :] + time_step * half
        )


def with_charge(dst, src, begin, charges, places):
    dst[0 : 3 * places, :] = src[begin : begin + 3 * places, :]
    dst[3 * places : 4 * places, :] = charges


def moved_self_kernel(moved, pos, force_out, full, cols):
    places = pos.shape[0] // 4
    with_charge(full, moved, 0, pos[3 * places : 4 * places, :], places)
    cols[0] = jnp.transpose(full[...])
    force_out[...] = jnp.zeros_like(force_out)
    add_self(force_out, full, cols, places)


def moved_near_kernel(moved, up, down, pos, up_pk, down_pk, force_in, work_near, force_out, full, cols):
    places = pos.shape[0] // 4
    rows = 4 * places
    at = 2 * NE + 3 * places
    force_out[...] = force_in[...]
    for n, (src, charges) in enumerate(
        (
            (down, down_pk[at : at + places, :]),
            (up, up_pk[at : at + places, :]),
            (moved, pos[3 * places : rows, :]),
        )
    ):
        with_charge(full, src, 0, charges, places)
        cols[(0, 2, 1)[n]] = jnp.transpose(full[...])
    add_listed(force_out, full, cols, work_near, places, lambda blk: blk - 3)


def moved_far_kernel(
    moved, low, high, pos, low_pk, high_pk, force_in, work_far, work_below, half, masses,
    shown, speed, force, full, cols
):
    places = pos.shape[0] // 4
    rows = 4 * places
    force[...] = force_in[...]
    for n, (src, pack) in enumerate(((low, low_pk), (high, high_pk))):
        for k in range(3):
            at = 2 * NS + k * rows + 3 * places
            with_charge(full, src, 3 * places * k, pack[at : at + places, :], places)
            cols[3 * n + k] = jnp.transpose(full[...])
    with_charge(full, moved, 0, pos[3 * places : rows, :], places)
    add_listed(force, full, cols, work_far, places, lambda blk: blk - 3)
    add_listed(force, full, cols, work_below, places, lambda blk: blk)
    inverse = time_step * (1.0 / masses[...])
    for c in range(3):
        before = half[c]
        after = before + inverse * folded_force(force, full, places, c)
        speed[c] = after
        shown[c] = time_step * (before + after)


def call(kernel, outs, scratch, *args, flops=0, smem=(), smem_out=(), name=None):
    vmem = pl.BlockSpec(memory_space=pltpu.VMEM)
    scalar = pl.BlockSpec(memory_space=pltpu.SMEM)
    return pl.pallas_call(
        kernel,
        out_shape=outs,
        in_specs=[scalar if n in smem else vmem for n in range(len(args))],
        out_specs=[scalar if n in smem_out else vmem for n in range(len(outs))],
        scratch_shapes=scratch,
        cost_estimate=pl.CostEstimate(flops=flops, transcendentals=0, bytes_accessed=1 << 20),
        compiler_params=pltpu.CompilerParams(vmem_limit_bytes=60 * 1024 * 1024),
        name=name,
    )(*args)


def shifted(x, axis, distance):
    size = lax.axis_size(axis)
    return lax.ppermute(x, axis, [(i, (i + distance) % size) for i in range(size)])


def local(
    cells, offsets, charges, masses, velocity, task_first, task_second, task_count, kernel_taps
):
    cells, offsets, velocity = cells[:, 0, 0], offsets[:, 0, 0], velocity[:, 0, 0]
    charges, masses = charges[0, 0], masses[0, 0]
    places, atoms = charges.shape
    depth = places * PZ
    strips = lax.axis_size("grp")
    slots = task_first.shape[2]
    terms = kernel_taps.shape[0]
    rows = 4 * places
    number_far = strips - 3
    shape = jax.ShapeDtypeStruct
    vm = pltpu.VMEM

    pack = shape((2 * NE + rows + 8, 128), f32)
    own, pk_lo, pk_hi, pos, lists = call(
        spread_kernel,
        [shape((XO * YR, depth), f32), pack, pack, shape((rows, 128), f32), shape((8, 128), f32)],
        [vm((depth + 2 * PZ, 256), f32)],
        cells, offsets, charges, task_first[0], task_second[0], task_count,
        name="spread",
    )
    up = shifted(pk_lo, "grp", -1)
    down = shifted(pk_hi, "grp", 1)
    far = [shifted(lists, "grp", d) for d in range(2, strips - 1)]

    force_shape = shape((3 * places * 8, 128), f32)
    table_shape = (2, XW * YR, terms * 256)
    line, edge_table, partial, force = call(
        tables_kernel,
        [
            shape((2, terms, depth, depth), bf16),
            shape(table_shape, bf16),
            shape((XW * YR, depth), f32),
            force_shape,
        ],
        [
            vm((8, 128), f32),
            vm(table_shape, bf16),
            vm((2, terms * 256, depth), bf16),
            vm((1, 128, 128), f32),
            vm(force_shape.shape, f32),
        ],
        kernel_taps, own, pos,
        flops=10**10, name="tables",
    )

    pack = shape((2 * NS + 3 * rows + 8 * strips, 128), f32)
    edge = shape((2 * N2, 128), f32)
    to_low, to_high, edge_low, edge_high, mid = call(
        functools.partial(planes_kernel, number_far=number_far),
        [pack, pack, edge, edge, shape((XO * YR, depth), f32)],
        [vm((2, terms * 256, depth), bf16)],
        up, down, pos, lists, *far, line, edge_table, partial,
        name="planes",
    )
    high = shifted(to_low, "patch", -1)
    low = shifted(to_high, "patch", 1)
    e_hi = shifted(edge_low, "patch", -2)
    e_lo = shifted(edge_high, "patch", 2)

    work = shape((4 * strips * slots + 8,), i32)
    force, work_near, work_far = call(
        functools.partial(near_kernel, number_far=number_far, strips=strips),
        [force_shape, work, work],
        [pltpu.SMEM((strips, 8, 128), f32), vm((3, 128, 128), f32), pltpu.SemaphoreType.DMA((strips,))],
        up, down, pos, lists, *far, force,
        flops=10**10, smem_out=(1, 2), name="near",
    )

    half, moved, work_below = call(
        functools.partial(sample_kernel, strips=strips),
        [shape((3, places, atoms), f32), shape((3 * places, 128), f32), work],
        [
            vm(force_shape.shape, f32),
            pltpu.SMEM((strips, 8, 128), f32),
            vm((6, 128, 128), f32),
            vm((XO * YR, depth), f32),
            vm((depth + 2 * PZ, XO * YR), f32),
            vm((3, places, atoms), f32),
            pltpu.SemaphoreType.DMA((strips,)),
        ],
        cells, offsets, charges, masses, velocity, pos, mid, low, high, e_lo, e_hi, force, work_far,
        smem=(12,), smem_out=(2,), name="sample",
    )

    moved_up = shifted(moved, "grp", -1)
    moved_down = shifted(moved, "grp", 1)
    force = call(
        moved_self_kernel,
        [force_shape],
        [vm((rows, 128), f32), vm((1, 128, 128), f32)],
        moved, pos,
        flops=10**10, name="moved_self",
    )[0]
    column = jnp.concatenate([moved_down, moved, moved_up], axis=0)
    moved_high = shifted(column, "patch", -1)
    moved_low = shifted(column, "patch", 1)
    force = call(
        moved_near_kernel,
        [force_shape],
        [vm((rows, 128), f32), vm((3, 128, 128), f32)],
        moved, moved_up, moved_down, pos, up, down, force, work_near,
        smem=(7,), flops=10**10, name="moved_near",
    )[0]
    shown, speed = call(
        moved_far_kernel,
        [shape((3, places, atoms), f32)] * 2,
        [vm(force_shape.shape, f32), vm((rows, 128), f32), vm((6, 128, 128), f32)],
        moved, moved_low, moved_high, pos, low, high, force, work_far, work_below, half, masses,
        smem=(7, 8), name="moved_far",
    )
    return shown[:, None, None], speed[:, None, None]


def solution(mesh):
    placed = (
        P(None, "patch", "grp", None, None),
        P(None, "patch", "grp", None, None),
        P("patch", "grp", None, None),
        P("patch", "grp", None, None),
        P(None, "patch", "grp", None, None),
        P("patch", "grp", None),
        P("patch", "grp", None),
        P("patch", "grp"),
        P(),
    )
    return jax.shard_map(
        local,
        mesh=mesh,
        in_specs=placed,
        out_specs=(P(None, "patch", "grp", None, None), P(None, "patch", "grp", None, None)),
        check_vma=False,
    )
```

profile of v0, /device:TPU:3, one launch (start us, length us, event | category | flops | bytes accessed | tf_op | source)
XLA Modules:
  0.0 90.0 jit_solution(4690392016851211001)
XLA Ops:
  1.3 3.8 %spread.1 = (f32[240,256]{1,0:T(8,128)}, f32[344,128]{1,0:T(8,128)}, f32[344,128]{1,0:T(8,128)}, f32[128,128]{1,0:T(8,128)}, f32[8,128]{1,0:T(8,128)}) custom-call(s32[3,32,128]{2,1,0:T(8,128)} %bitcast.13, f32[3,32,128]{2,1,0:T(8,128)} %bitcast.15, f32[32,128]{1,0:T(8,128)} %bitcast.19, s32[1,32]{1,0:T(1,128)} %bitcast.22, s32[1,32]{1,0:T(1,128)} %bitcast.23, ...), custom_call_target="tpu_custom_call" | custom-call | bytes 1048576 | tf_op jit(solution)/shard_map/spread/pallas_call | solution.py:530
  5.1 2.3 %collective-permute-start.2 = (f32[8,128]{1,0:T(8,128)}, f32[8,128]{1,0:T(8,128)S(1)}, u32[]{:S(2)}, u32[]{:S(2)}) collective-permute-start(f32[8,128]{1,0:T(8,128)} %get-tuple-element.27.refs_3_), channel_id=1, source_target_pairs={{0,2},{1,3},{2,0},{3,1},{4,6},{5,7},{6,4},{7,5},{8,10},{9,11},{10,... | collective-permute-start | bytes 12296 | tf_op jit(solution)/shard_map/ppermute | solution.py:544
  7.4 1.1 %collective-permute-start = (f32[344,128]{1,0:T(8,128)}, f32[344,128]{1,0:T(8,128)S(1)}, u32[]{:S(2)}, u32[]{:S(2)}) collective-permute-start(f32[344,128]{1,0:T(8,128)} %get-tuple-element.25), channel_id=1, source_target_pairs={{0,3},{1,0},{2,1},{3,2},{4,7},{5,4},{6,5},{7,6},{8,11},{9,8},{10,9... | collective-permute-start | bytes 528392 | tf_op jit(solution)/shard_map/ppermute | solution.py:544
  8.5 0.4 collective-permute-start.1
  8.9 14.3 %tables.1 = (bf16[2,6,256,256]{3,2,1,0:T(8,128)(2,1)}, bf16[2,624,1536]{2,1,0:T(8,128)(2,1)}, f32[624,256]{1,0:T(8,128)}, f32[768,128]{1,0:T(8,128)}) custom-call(f32[6,17]{1,0:T(8,128)} %taps_in.1, f32[240,256]{1,0:T(8,128)} %get-tuple-element.28.own, f32[128,128]{1,0:T(8,128)} %get-tuple-element.24.pos.refs_2_), custom_call_target="tpu_custom_call" | custom-call | flops 10000000000 | bytes 1048576 | tf_op jit(solution)/shard_map/tables/pallas_call | solution.py:530
  23.1 0.0 collective-permute-done.2.refs_4_
  23.2 0.0 collective-permute-done.refs_0_.up_pk
  23.2 0.0 copy-start.3
  23.2 0.0 collective-permute-done.1.refs_1_.down_pk
  23.2 0.0 copy-start.4
  23.2 0.6 copy-done.11
  23.7 0.1 copy-done.3
  23.8 0.1 copy-done.4
  23.9 6.1 %planes.1 = (f32[784,128]{1,0:T(8,128)}, f32[784,128]{1,0:T(8,128)}, f32[80,128]{1,0:T(8,128)}, f32[80,128]{1,0:T(8,128)}, f32[240,256]{1,0:T(8,128)}) custom-call(f32[344,128]{1,0:T(8,128)} %copy-done.3, f32[344,128]{1,0:T(8,128)} %copy-done.4, f32[128,128]{1,0:T(8,128)} %get-tuple-element.24.pos.refs_2_, f32[8,128]{1,0:T(8,128)} %get-tuple-element.27.refs_3_, ...), custom_call_target="tpu_custom_call" | custom-call | bytes 1048576 | tf_op jit(solution)/shard_map/planes/pallas_call | solution.py:530
  30.0 1.2 %collective-permute-start.5 = (f32[80,128]{1,0:T(8,128)}, f32[80,128]{1,0:T(8,128)S(1)}, u32[]{:S(2)}, u32[]{:S(2)}) collective-permute-start(f32[80,128]{1,0:T(8,128)} %get-tuple-element.35), channel_id=1, source_target_pairs={{0,8},{4,12},{8,16},{12,20},{16,24},{20,28},{24,0},{28,4},{1,9},{5... | collective-permute-start | bytes 122888 | tf_op jit(solution)/shard_map/ppermute | solution.py:544
  31.2 0.3 collective-permute-start.6
  31.4 4.1 %collective-permute-start.3 = (f32[784,128]{1,0:T(8,128)}, f32[784,128]{1,0:T(8,128)S(1)}, u32[]{:S(2)}, u32[]{:S(2)}) collective-permute-start(f32[784,128]{1,0:T(8,128)} %get-tuple-element.33), channel_id=1, source_target_pairs={{0,4},{4,8},{8,12},{12,16},{16,20},{20,24},{24,28},{28,0},{1,5},{5... | collective-permute-start | bytes 1204232 | tf_op jit(solution)/shard_map/ppermute | solution.py:544
  35.5 0.0 collective-permute-start.4
  35.5 9.1 %near.1 = (f32[768,128]{1,0:T(8,128)}, s32[520]{0:T(1024)}, s32[520]{0:T(1024)}) custom-call(f32[344,128]{1,0:T(8,128)} %copy-done.3, f32[344,128]{1,0:T(8,128)} %copy-done.4, f32[128,128]{1,0:T(8,128)} %get-tuple-element.24.pos.refs_2_, f32[8,128]{1,0:T(8,128)} %get-tuple-element.27.refs_3_, f32[8,128]{1,0:T(8,128)} %copy-done.11, ...), custom_call_target="tpu_custom_call" | custom-call | flops 10000000000 | bytes 1048576 | tf_op jit(solution)/shard_map/near/pallas_call | solution.py:530
  44.6 0.0 collective-permute-done.5.e_lo
  44.6 0.0 copy-start.9
  44.7 0.0 collective-permute-done.6.e_hi
  44.7 0.0 copy-start.10
  44.7 0.2 collective-permute-done.3.low.low_pk
  44.9 1.1 %collective-permute-done.4.high.high_pk = f32[784,128]{1,0:T(8,128)S(1)} collective-permute-done((f32[784,128]{1,0:T(8,128)}, f32[784,128]{1,0:T(8,128)S(1)}, u32[]{:S(2)}, u32[]{:S(2)}) %collective-permute-start.4) | collective-permute-done | bytes 401440 | tf_op jit(solution)/shard_map/ppermute | solution.py:544
  46.0 0.0 copy-done.9
  46.0 0.0 copy-done.10
  46.0 0.0 copy-done
  46.0 0.8 copy-done.1
  46.8 12.8 %sample.1 = (f32[3,32,128]{2,1,0:T(8,128)}, f32[96,128]{1,0:T(8,128)}, s32[520]{0:T(1024)}) custom-call(s32[3,32,128]{2,1,0:T(8,128)} %bitcast.14, f32[3,32,128]{2,1,0:T(8,128)} %bitcast.16, f32[32,128]{1,0:T(8,128)} %bitcast.20, f32[32,128]{1,0:T(8,128)} %bitcast.17, f32[3,32,128]{2,1,0:T(8,128)} %bitcast.21, f32[128,128]{1,0:T(8,128)} %get-tuple-element.24.pos.refs_2_, ...), custom_call_target="tpu_custom_call" | custom-call | bytes 1048576 | tf_op jit(solution)/shard_map/sample/pallas_call | solution.py:530
  59.5 0.0 copy-start.2
  59.5 0.8 collective-permute-start.8
  60.4 0.7 collective-permute-start.7
  61.1 9.3 %moved_self.1.force_in = f32[768,128]{1,0:T(8,128)} custom-call(f32[96,128]{1,0:T(8,128)} %get-tuple-element.40.moved, f32[128,128]{1,0:T(8,128)} %get-tuple-element.24.pos.refs_2_), custom_call_target="tpu_custom_call" | custom-call | flops 10000000000 | bytes 1048576 | tf_op jit(solution)/shard_map/moved_self/pallas_call | solution.py:530
  70.4 0.0 collective-permute-done.7.down
  70.4 0.0 copy-done.2
  70.4 0.0 collective-permute-done.8.up
  70.4 0.0 copy-start.7
  70.4 3.3 %collective-permute-start.10 = (f32[288,128]{1,0:T(8,128)S(1)}, f32[288,128]{1,0:T(8,128)S(1)}, u32[]{:S(2)}, u32[]{:S(2)}) collective-permute-start(f32[288,128]{1,0:T(8,128)S(1)} %constant_dynamic-update-slice_fusion), channel_id=1, source_target_pairs={{0,28},{4,0},{8,4},{12,8},{16,12},{20,16},{24,20},{28,24},{1,29},{... | collective-permute-start | bytes 442376 | tf_op jit(solution)/shard_map/ppermute | solution.py:544
  73.7 0.0 collective-permute-start.9
  73.7 0.0 copy-done.7
  73.7 6.4 %moved_near.1.force_in = f32[768,128]{1,0:T(8,128)} custom-call(f32[96,128]{1,0:T(8,128)} %get-tuple-element.40.moved, f32[96,128]{1,0:T(8,128)} %copy-done.7, f32[96,128]{1,0:T(8,128)} %copy-done.8, f32[128,128]{1,0:T(8,128)} %get-tuple-element.24.pos.refs_2_, f32[344,128]{1,0:T(8,128)} %copy-done.3, f32[344,128]{1,0:T(8,128)} %copy-done.4, ...), custom_call_target="tpu_custom_call" | custom-call | flops 10000000000 | bytes 1048576 | tf_op jit(solution)/shard_map/moved_near/pallas_call | solution.py:530
  80.1 0.0 collective-permute-done.10.high
  80.1 0.0 collective-permute-done.9.low
  80.1 0.0 copy-start.6
  80.1 0.6 copy-done.5
  80.8 0.1 copy-done.6
  80.9 9.2 %moved_far.1 = (f32[3,32,128]{2,1,0:T(8,128)}, f32[3,32,128]{2,1,0:T(8,128)}) custom-call(f32[96,128]{1,0:T(8,128)} %get-tuple-element.40.moved, f32[288,128]{1,0:T(8,128)} %copy-done.6, f32[288,128]{1,0:T(8,128)} %copy-done.5, f32[128,128]{1,0:T(8,128)} %get-tuple-element.24.pos.refs_2_, f32[784,128]{1,0:T(8,128)} %copy-done, f32[784,128]{1,0:T(8,128)} %copy-done.1, ...), custom_call_target="tpu_custom_call" | custom-call | bytes 1048576 | tf_op jit(solution)/shard_map/moved_far/pallas_call | solution.py:530
  (9 shorter events, 0.0 us)
Async XLA Ops:
  5.1 18.0 %collective-permute-start.2 = (f32[8,128]{1,0:T(8,128)}, f32[8,128]{1,0:T(8,128)S(1)}, u32[]{:S(2)}, u32[]{:S(2)}) collective-permute-start(f32[8,128]{1,0:T(8,128)} %get-tuple-element.27.refs_3_), channel_id=1, source_target_pairs={{0,2},{1,3},{2,0},{3,1},{4,6},{5,7},{6,4},{7,5},{8,10},{9,11},{10,... | collective-permute-start | bytes 12296 | tf_op jit(solution)/shard_map/ppermute | solution.py:544
  7.4 15.7 %collective-permute-start = (f32[344,128]{1,0:T(8,128)}, f32[344,128]{1,0:T(8,128)S(1)}, u32[]{:S(2)}, u32[]{:S(2)}) collective-permute-start(f32[344,128]{1,0:T(8,128)} %get-tuple-element.25), channel_id=1, source_target_pairs={{0,3},{1,0},{2,1},{3,2},{4,7},{5,4},{6,5},{7,6},{8,11},{9,8},{10,9... | collective-permute-start | bytes 528392 | tf_op jit(solution)/shard_map/ppermute | solution.py:544
  8.5 14.7 %collective-permute-start.1 = (f32[344,128]{1,0:T(8,128)}, f32[344,128]{1,0:T(8,128)S(1)}, u32[]{:S(2)}, u32[]{:S(2)}) collective-permute-start(f32[344,128]{1,0:T(8,128)} %get-tuple-element.26), channel_id=1, source_target_pairs={{0,1},{1,2},{2,3},{3,0},{4,5},{5,6},{6,7},{7,4},{8,9},{9,10},{10,1... | collective-permute-start | bytes 528392 | tf_op jit(solution)/shard_map/ppermute | solution.py:544
  23.2 0.6 copy-start.11
  23.2 0.7 copy-start.3
  23.2 0.7 copy-start.4
  30.0 14.7 %collective-permute-start.5 = (f32[80,128]{1,0:T(8,128)}, f32[80,128]{1,0:T(8,128)S(1)}, u32[]{:S(2)}, u32[]{:S(2)}) collective-permute-start(f32[80,128]{1,0:T(8,128)} %get-tuple-element.35), channel_id=1, source_target_pairs={{0,8},{4,12},{8,16},{12,20},{16,24},{20,28},{24,0},{28,4},{1,9},{5... | collective-permute-start | bytes 122888 | tf_op jit(solution)/shard_map/ppermute | solution.py:544
  31.2 13.5 %collective-permute-start.6 = (f32[80,128]{1,0:T(8,128)}, f32[80,128]{1,0:T(8,128)S(1)}, u32[]{:S(2)}, u32[]{:S(2)}) collective-permute-start(f32[80,128]{1,0:T(8,128)} %get-tuple-element.36), channel_id=1, source_target_pairs={{0,24},{4,28},{8,0},{12,4},{16,8},{20,12},{24,16},{28,20},{1,25},{... | collective-permute-start | bytes 122888 | tf_op jit(solution)/shard_map/ppermute | solution.py:544
  31.4 13.5 %collective-permute-start.3 = (f32[784,128]{1,0:T(8,128)}, f32[784,128]{1,0:T(8,128)S(1)}, u32[]{:S(2)}, u32[]{:S(2)}) collective-permute-start(f32[784,128]{1,0:T(8,128)} %get-tuple-element.33), channel_id=1, source_target_pairs={{0,4},{4,8},{8,12},{12,16},{16,20},{20,24},{24,28},{28,0},{1,5},{5... | collective-permute-start | bytes 1204232 | tf_op jit(solution)/shard_map/ppermute | solution.py:544
  35.5 10.5 %collective-permute-start.4 = (f32[784,128]{1,0:T(8,128)}, f32[784,128]{1,0:T(8,128)S(1)}, u32[]{:S(2)}, u32[]{:S(2)}) collective-permute-start(f32[784,128]{1,0:T(8,128)} %get-tuple-element.34), channel_id=1, source_target_pairs={{0,28},{4,0},{8,4},{12,8},{16,12},{20,16},{24,20},{28,24},{1,29},{... | collective-permute-start | bytes 1204232 | tf_op jit(solution)/shard_map/ppermute | solution.py:544
  44.6 1.4 %copy-start.9 = (f32[80,128]{1,0:T(8,128)}, f32[80,128]{1,0:T(8,128)S(1)}, u32[]{:S(2)}) copy-start(f32[80,128]{1,0:T(8,128)S(1)} %collective-permute-done.5.e_lo) | copy-start | bytes 122884
  44.7 1.3 %copy-start.10 = (f32[80,128]{1,0:T(8,128)}, f32[80,128]{1,0:T(8,128)S(1)}, u32[]{:S(2)}) copy-start(f32[80,128]{1,0:T(8,128)S(1)} %collective-permute-done.6.e_hi) | copy-start | bytes 122884
  44.9 1.1 %copy-start = (f32[784,128]{1,0:T(8,128)}, f32[784,128]{1,0:T(8,128)S(1)}, u32[]{:S(2)}) copy-start(f32[784,128]{1,0:T(8,128)S(1)} %collective-permute-done.3.low.low_pk) | copy-start | bytes 1204228
  46.0 0.8 copy-start.1
  59.5 10.8 %copy-start.2 = (f32[96,128]{1,0:T(8,128)S(1)}, f32[96,128]{1,0:T(8,128)}, u32[]{:S(2)}) copy-start(f32[96,128]{1,0:T(8,128)} %get-tuple-element.40.moved) | copy-start | bytes 147460
  59.5 10.9 %collective-permute-start.8 = (f32[96,128]{1,0:T(8,128)}, f32[96,128]{1,0:T(8,128)S(1)}, u32[]{:S(2)}, u32[]{:S(2)}) collective-permute-start(f32[96,128]{1,0:T(8,128)} %get-tuple-element.40.moved), channel_id=1, source_target_pairs={{0,3},{1,0},{2,1},{3,2},{4,7},{5,4},{6,5},{7,6},{8,11},{9,8},{10,9... | collective-permute-start | bytes 147464 | tf_op jit(solution)/shard_map/ppermute | solution.py:544
  60.4 10.0 %collective-permute-start.7 = (f32[96,128]{1,0:T(8,128)}, f32[96,128]{1,0:T(8,128)S(1)}, u32[]{:S(2)}, u32[]{:S(2)}) collective-permute-start(f32[96,128]{1,0:T(8,128)} %get-tuple-element.40.moved), channel_id=1, source_target_pairs={{0,1},{1,2},{2,3},{3,0},{4,5},{5,6},{6,7},{7,4},{8,9},{9,10},{10,1... | collective-permute-start | bytes 147464 | tf_op jit(solution)/shard_map/ppermute | solution.py:544
  70.4 3.3 %copy-start.8 = (f32[96,128]{1,0:T(8,128)}, f32[96,128]{1,0:T(8,128)S(1)}, u32[]{:S(2)}) copy-start(f32[96,128]{1,0:T(8,128)S(1)} %collective-permute-done.7.down) | copy-start | bytes 147460
  70.4 3.3 %copy-start.7 = (f32[96,128]{1,0:T(8,128)}, f32[96,128]{1,0:T(8,128)S(1)}, u32[]{:S(2)}) copy-start(f32[96,128]{1,0:T(8,128)S(1)} %collective-permute-done.8.up) | copy-start | bytes 147460
  70.4 9.7 %collective-permute-start.10 = (f32[288,128]{1,0:T(8,128)S(1)}, f32[288,128]{1,0:T(8,128)S(1)}, u32[]{:S(2)}, u32[]{:S(2)}) collective-permute-start(f32[288,128]{1,0:T(8,128)S(1)} %constant_dynamic-update-slice_fusion), channel_id=1, source_target_pairs={{0,28},{4,0},{8,4},{12,8},{16,12},{20,16},{24,20},{28,24},{1,29},{... | collective-permute-start | bytes 442376 | tf_op jit(solution)/shard_map/ppermute | solution.py:544
  73.7 6.4 %collective-permute-start.9 = (f32[288,128]{1,0:T(8,128)S(1)}, f32[288,128]{1,0:T(8,128)S(1)}, u32[]{:S(2)}, u32[]{:S(2)}) collective-permute-start(f32[288,128]{1,0:T(8,128)S(1)} %constant_dynamic-update-slice_fusion), channel_id=1, source_target_pairs={{0,4},{4,8},{8,12},{12,16},{16,20},{20,24},{24,28},{28,0},{1,5},{5... | collective-permute-start | bytes 442376 | tf_op jit(solution)/shard_map/ppermute | solution.py:544
  80.1 0.7 copy-start.5
  80.1 0.7 copy-start.6
where the time goes:
time: 90.9 us; the launch traced here: 90 us
  Pallas kernels  70.9 us (78%)
  starting transfers between devices  14.1 us (16%)
  local copies, waits for them, and re-layouts  2.24 us (2%)
  between operations  1.44 us (2%)
  waiting for transfers between devices  1.34 us (1%)
    pallas_call x8, Pallas kernels, call(): pl.pallas_call(kernel, out_shape=outs, in_specs=[scalar if n in smem else...  70.9 us
    ppermute x11, starting transfers between devices, shifted(): lax.ppermute(x, axis, [(i, (i + distance) % size) for i in range(size)])  14.1 us
    unnamed x26, local copies, waits for them, and re-layouts  2.23 us
  transfers between devices with their start and end apart: 11, of which 2 were waited for; matrix products, arithmetic and copies ran while one was open for 0% of the time, Pallas kernels for 43%

commit v1 on v0

--- a/solution.py
+++ b/solution.py
@@ -25,6 +25,8 @@
 NE = 104
 NS = 184
 N2 = 40
+
+UNROLL = 4
 
 f32 = jnp.float32
 bf16 = jnp.bfloat16
@@ -131,23 +133,62 @@
             pk_hi[dst, :] = own[x * YR + YO - YE : x * YR + YO, lanes]
 
 
-def add_side(force, posr, cols, blk, r, p, places, offsets):
-    off_x, off_y, off_z = offsets
+def fill_receivers(parts, posr, places):
+    rows = iota((8, 128), 0)
+    for c in range(3):
+        base = 8 * (places + 1) * c
+        constant = jnp.where(rows == c, -1.0, 0.0)
+        for r in range(places + 1):
+            parts[base + 8 * r : base + 8 * r + 8, :] = constant
+        for g in range(0, places, 8):
+            x = posr[c * places + g : c * places + g + 8, :]
+            hi = x.astype(bf16).astype(f32)
+            rest = x - hi
+            mid = rest.astype(bf16).astype(f32)
+            for n, value in enumerate((hi, mid, rest - mid)):
+                parts[pl.ds(base + 8 * g + 4 + n, 8, stride=8), :] = value
+
+
+def side_operands(parts, src, source, r, shifts):
+    rows = iota((8, 128), 0)
+    shift_x, shift_y, shift_z = shifts
+    shift = jnp.where(rows == 0, shift_x, jnp.where(rows == 1, shift_y, shift_z))
+    at = src[pl.ds(pl.multiple_of(8 * source, 8), 8), :]
+    at = jnp.where(rows < 3, at - shift, at)
+    hi = at.astype(bf16).astype(f32)
+    rest = at - hi
+    mid = rest.astype(bf16).astype(f32)
+    low = rest - mid
+    mid = pltpu.roll(mid, 4, 0)
+    left = jnp.concatenate(
+        [jnp.where(rows < 4, hi, mid), jnp.where(rows < 4, low, 1.0)], axis=0
+    )
+    top = []
+    end = []
+    for c in range(4):
+        sign = 1.0 if c == 3 else -1.0
+        top.append(jnp.where((rows & 3) == c, sign, 0.0))
+        if c < 3:
+            end.append(parts[pl.ds(pl.multiple_of(parts.shape[0] // 3 * c + 8 * r, 8), 8), :])
+        else:
+            end.append(jnp.where(rows == c, sign, 0.0))
+    right = jnp.concatenate(
+        [jnp.concatenate(top, axis=1), jnp.concatenate(end, axis=1)], axis=0
+    )
+    return jnp.transpose(left).astype(bf16), right.astype(bf16)
+
+
+def side_push(force, pairs, r):
     shape = (8, 128)
-    xr = jnp.broadcast_to(posr[pl.ds(r, 1), :] + off_x, shape)
-    yr = jnp.broadcast_to(posr[pl.ds(places + r, 1), :] + off_y, shape)
-    zr = jnp.broadcast_to(posr[pl.ds(2 * places + r, 1), :] + off_z, shape)
     ax = jnp.zeros(shape, f32)
     ay = jnp.zeros(shape, f32)
     az = jnp.zeros(shape, f32)
-    ix = jnp.full(shape, p, i32)
-    iy, iz, iq = ix + places, ix + 2 * places, ix + 3 * places
     for k in range(16):
-        col = cols[blk, 8 * k : 8 * k + 8, :]
-        dx = xr - jnp.take_along_axis(col, ix, axis=1)
-        dy = yr - jnp.take_along_axis(col, iy, axis=1)
-        dz = zr - jnp.take_along_axis(col, iz, axis=1)
-        qs = jnp.take_along_axis(col, iq, axis=1)
+        rows = slice(8 * k, 8 * k + 8)
+        dx = pairs[rows, 0:128]
+        dy = pairs[rows, 128:256]
+        dz = pairs[rows, 256:384]
+        qs = pairs[rows, 384:512]
         soft = (dx * dx + dy * dy) + (dz * dz + 1.0)
         reach = jnp.maximum(soft_end - soft, 0.0)
         rs = lax.rsqrt(soft)
@@ -157,28 +198,71 @@
         ay = ay + c * dy
         az = az + c * dz
     for c, a in enumerate((ax, ay, az)):
-        rows = pl.ds(pl.multiple_of((c * places + r) * 8, 8), 8)
+        rows = pl.ds(pl.multiple_of((3 * r + c) * 8, 8), 8)
         force[rows, :] += a
 
 
-def folded_force(force, posr, places, c):
-    part = force[c * places * 8 : (c + 1) * places * 8, :]
-    total = jnp.sum(part.reshape(places, 8, 128), axis=1)
-    return total * (posr[3 * places : 4 * places, :] * push_scale)
-
-
-def add_self(force, posr, cols, places):
-    def body(r, carry):
-        add_side(force, posr, cols, 0, r, r, places, (0.0, 0.0, 0.0))
+def add_sides(force, parts, src, pairs, number, places, decode):
+    def prepare(n, dst):
+        r, source, shifts = decode(n)
+        left, right = side_operands(parts, src, source, r, shifts)
+        dst[...] = dot(left, right)
+
+    def receiver(n):
+        return jnp.where(n < number, decode(n)[0], places)
+
+    for u, dst in enumerate(pairs):
+        prepare(jnp.int32(u), dst)
+
+    def body(m, carry):
+        n = UNROLL * m
+        for u, dst in enumerate(pairs):
+            side_push(force, dst, receiver(n + u))
+            prepare(n + UNROLL + u, dst)
         return carry
 
-    lax.fori_loop(0, places, body, 0)
-
-
-def add_listed(force, posr, cols, work, places, slot_of):
+    lax.fori_loop(0, (number + UNROLL - 1) // UNROLL, body, 0)
+
+
+def fill_sources(src, block, component, places):
+    for c in range(4):
+        rows = component(c)
+        for g in range(0, places, 8):
+            at = (block * places + g) * 8 + c
+            src[pl.ds(at, 8, stride=8), :] = rows[g : g + 8, :]
+
+
+def rows_of(ref, begin, places):
+    return lambda c: ref[begin + c * places : begin + (c + 1) * places, :]
+
+
+def moved_rows(ref, begin, charges, at, places):
+    return lambda c: (
+        charges[at + 3 * places : at + 4 * places, :]
+        if c == 3
+        else ref[begin + c * places : begin + (c + 1) * places, :]
+    )
+
+
+def folded_force(force, posr, places):
+    part = force[0 : 24 * places, :].reshape(places, 3, 8, 128)
+    total = jnp.sum(part, axis=2)
+    scale = posr[3 * places : 4 * places, :] * push_scale
+    return [total[:, c, :] * scale for c in range(3)]
+
+
+def add_self(force, parts, src, pairs, places):
+    def decode(n):
+        n = jnp.minimum(n, places - 1)
+        return n, n, (0.0, 0.0, 0.0)
+
+    add_sides(force, parts, src, pairs, places, places, decode)
+
+
+def add_listed(force, parts, src, pairs, work, places, first_block):
     bits = places.bit_length() - 1
 
-    def body(n, carry):
+    def decode(n):
         code = work[n + 1]
         r = code & (places - 1)
         p = (code >> bits) & (places - 1)
@@ -186,15 +270,17 @@
         dslab = blk // 3 - 1
         dstrip = blk % 3 - 1
         dz = ((r - p + 1) & (places - 1)) - 1
-        off = (
+        shifts = (
             (-MXD * dslab).astype(f32),
             (-MYD * dstrip).astype(f32),
             (PZ * dz).astype(f32),
         )
-        add_side(force, posr, cols, slot_of(blk), r, p, places, off)
-        return carry
-
-    lax.fori_loop(0, work[0], body, 0)
+        source = jnp.maximum(blk - first_block, 0) * places + p
+        return r, source, shifts
+
+    @pl.when(work[0] > 0)
+    def _():
+        add_sides(force, parts, src, pairs, work[0], places, decode)
 
 
 def wrap_step(delta, count):
@@ -237,9 +323,10 @@
         return lax.fori_loop(0, live, each, carry)
 
     near, far = lax.fori_loop(0, number, each_list, (jnp.int32(0), jnp.int32(0)))
-    work_far[0] = far
-    if not below:
-        work_near[0] = near
+    for work, number in ((work_far, far),) + (() if below else ((work_near, near),)):
+        work[0] = number
+        for n in range(UNROLL * 2):
+            work[number + 1 + n] = jnp.int32(0)
 
 
 def tap_lookup(taps, t, index):
@@ -286,7 +373,7 @@
 
 
 def tables_kernel(
-    taps_in, own, pos, line, edge_table, partial, force_out, taps, table, smooth, cols, force
+    taps_in, own, pos, line, edge_table, partial, force_out, taps, table, smooth, src, parts, *pairs
 ):
     places = pos.shape[0] // 4
     depth = places * PZ
@@ -316,10 +403,10 @@
             edge_table, slice(None), slice(t * 256, t * 256 + 256), plane_table(taps, t, edge_x, edge_y)
         )
     partial[...] = dot3((table[0], table[1]), (smooth[0], smooth[1]))
-    cols[0] = jnp.transpose(pos[...])
-    force[...] = jnp.zeros_like(force)
-    add_self(force, pos, cols, places)
-    force_out[...] = force[...]
+    fill_sources(src, 0, rows_of(pos, 0, places), places)
+    fill_receivers(parts, pos, places)
+    force_out[...] = jnp.zeros_like(force_out)
+    add_self(force_out, parts, src, pairs, places)
 
 
 def planes_kernel(
@@ -373,7 +460,7 @@
     up, down, pos, lists = refs[:4]
     far = refs[4 : 4 + number_far]
     force_in = refs[4 + number_far]
-    force_out, work_near, work_far, held, cols, sem = refs[5 + number_far :]
+    force_out, work_near, work_far, held, src, parts, *pairs, sem = refs[5 + number_far :]
     places = pos.shape[0] // 4
     rows = 4 * places
     sources = [lists.at[0:8], down.at[pl.ds(2 * NE + rows, 8)], up.at[pl.ds(2 * NE + rows, 8)]]
@@ -384,18 +471,19 @@
     for copy in copies:
         copy.start()
     force_out[...] = force_in[...]
-    cols[0] = jnp.transpose(down[2 * NE : 2 * NE + rows, :])
-    cols[1] = jnp.transpose(pos[...])
-    cols[2] = jnp.transpose(up[2 * NE : 2 * NE + rows, :])
+    blocks = [rows_of(down, 2 * NE, places), rows_of(pos, 0, places), rows_of(up, 2 * NE, places)]
+    for n, block in enumerate(blocks):
+        fill_sources(src, n, block, places)
+    fill_receivers(parts, pos, places)
     for copy in copies:
         copy.wait()
     list_tasks(held, len(sources), False, work_near, work_far, places, strips)
-    add_listed(force_out, pos, cols, work_near, places, lambda blk: blk - 3)
+    add_listed(force_out, parts, src, pairs, work_near, places, 3)
 
 
 def sample_kernel(
     cells, frac, charge, masses, velocity, pos, mid, low, high, e_lo, e_hi, force_in, work_far,
-    half_out, moved, work_below, force, held, cols, grid, turned, long, sem, *, strips
+    half_out, moved, work_below, force, held, src, grid, turned, long, sem, parts, *pairs, strips
 ):
     places, atoms = charge.shape
     depth = places * PZ
@@ -410,8 +498,8 @@
     for x in range(XO):
         for half in range(2):
             lanes = slice(half * 128, half * 128 + 128)
-            src = pl.ds(half * NS + x * YO, YO)
-            value = mid[x * YR : x * YR + YO, lanes] + low[src, :] + high[src, :]
+            at_x = pl.ds(half * NS + x * YO, YO)
+            value = mid[x * YR : x * YR + YO, lanes] + low[at_x, :] + high[at_x, :]
             if x < 2:
                 value = value + e_lo[pl.ds(half * N2 + x * YO, YO), :]
             if x >= XO - 2:
@@ -450,20 +538,20 @@
             line = jnp.sum(value, axis=0, keepdims=True)
             long[c, 2 * m : 2 * m + 1, :] = line[:, :atoms]
             long[c, 2 * m + 1 : 2 * m + 2, :] = line[:, atoms:]
-    for n, src in enumerate((low, high)):
-        for k in range(3):
-            begin = 2 * NS + k * rows
-            cols[3 * n + k] = jnp.transpose(src[begin : begin + rows, :])
+    for n in range(6):
+        fill_sources(src, n, rows_of((low, high)[n // 3], 2 * NS + n % 3 * rows, places), places)
+    fill_receivers(parts, pos, places)
     force[...] = force_in[...]
-    add_listed(force, pos, cols, work_far, places, lambda blk: blk - 3)
+    add_listed(force, parts, src, pairs, work_far, places, 3)
     for copy in copies:
         copy.wait()
     list_tasks(held, strips, True, None, work_below, places, strips)
-    add_listed(force, pos, cols, work_below, places, lambda blk: blk)
+    add_listed(force, parts, src, pairs, work_below, places, 0)
     inverse = time_step * (1.0 / masses[...])
     q = charge[...]
+    short = folded_force(force, pos, places)
     for c in range(3):
-        total = folded_force(force, pos, places, c) - 2.0 * q * long[c]
+        total = short[c] - 2.0 * q * long[c]
         half = velocity[c] + inverse * total
         half_out[c] = half
         moved[c * places : (c + 1) * places, :] = (
@@ -471,55 +559,50 @@
         )
 
 
-def with_charge(dst, src, begin, charges, places):
-    dst[0 : 3 * places, :] = src[begin : begin + 3 * places, :]
-    dst[3 * places : 4 * places, :] = charges
-
-
-def moved_self_kernel(moved, pos, force_out, full, cols):
+def moved_self_kernel(moved, pos, force_out, src, parts, *pairs):
     places = pos.shape[0] // 4
-    with_charge(full, moved, 0, pos[3 * places : 4 * places, :], places)
-    cols[0] = jnp.transpose(full[...])
+    fill_sources(src, 0, moved_rows(moved, 0, pos, 0, places), places)
+    fill_receivers(parts, moved, places)
     force_out[...] = jnp.zeros_like(force_out)
-    add_self(force_out, full, cols, places)
-
-
-def moved_near_kernel(moved, up, down, pos, up_pk, down_pk, force_in, work_near, force_out, full, cols):
+    add_self(force_out, parts, src, pairs, places)
+
+
+def moved_near_kernel(
+    moved, up, down, pos, up_pk, down_pk, force_in, work_near, force_out, src, parts, *pairs
+):
     places = pos.shape[0] // 4
-    rows = 4 * places
-    at = 2 * NE + 3 * places
     force_out[...] = force_in[...]
-    for n, (src, charges) in enumerate(
-        (
-            (down, down_pk[at : at + places, :]),
-            (up, up_pk[at : at + places, :]),
-            (moved, pos[3 * places : rows, :]),
-        )
-    ):
-        with_charge(full, src, 0, charges, places)
-        cols[(0, 2, 1)[n]] = jnp.transpose(full[...])
-    add_listed(force_out, full, cols, work_near, places, lambda blk: blk - 3)
+    blocks = [
+        moved_rows(down, 0, down_pk, 2 * NE, places),
+        moved_rows(moved, 0, pos, 0, places),
+        moved_rows(up, 0, up_pk, 2 * NE, places),
+    ]
+    for n, block in enumerate(blocks):
+        fill_sources(src, n, block, places)
+    fill_receivers(parts, moved, places)
+    add_listed(force_out, parts, src, pairs, work_near, places, 3)
 
 
 def moved_far_kernel(
     moved, low, high, pos, low_pk, high_pk, force_in, work_far, work_below, half, masses,
-    shown, speed, force, full, cols
+    shown, speed, force, src, parts, *pairs
 ):
     places = pos.shape[0] // 4
     rows = 4 * places
     force[...] = force_in[...]
-    for n, (src, pack) in enumerate(((low, low_pk), (high, high_pk))):
-        for k in range(3):
-            at = 2 * NS + k * rows + 3 * places
-            with_charge(full, src, 3 * places * k, pack[at : at + places, :], places)
-            cols[3 * n + k] = jnp.transpose(full[...])
-    with_charge(full, moved, 0, pos[3 * places : rows, :], places)
-    add_listed(force, full, cols, work_far, places, lambda blk: blk - 3)
-    add_listed(force, full, cols, work_below, places, lambda blk: blk)
+    for n in range(6):
+        part, pack = ((low, low_pk), (high, high_pk))[n // 3]
+        k = n % 3
+        block = moved_rows(part, 3 * places * k, pack, 2 * NS + k * rows, places)
+        fill_sources(src, n, block, places)
+    fill_receivers(parts, moved, places)
+    add_listed(force, parts, src, pairs, work_far, places, 3)
+    add_listed(force, parts, src, pairs, work_below, places, 0)
+    short = folded_force(force, pos, places)
     inverse = time_step * (1.0 / masses[...])
     for c in range(3):
         before = half[c]
-        after = before + inverse * folded_force(force, full, places, c)
+        after = before + inverse * short[c]
         speed[c] = after
         shown[c] = time_step * (before + after)
 
@@ -534,7 +617,7 @@
         out_specs=[scalar if n in smem_out else vmem for n in range(len(outs))],
         scratch_shapes=scratch,
         cost_estimate=pl.CostEstimate(flops=flops, transcendentals=0, bytes_accessed=1 << 20),
-        compiler_params=pltpu.CompilerParams(vmem_limit_bytes=60 * 1024 * 1024),
+        compiler_params=pltpu.CompilerParams(vmem_limit_bytes=20 * 1024 * 1024),
         name=name,
     )(*args)
 
@@ -571,7 +654,12 @@
     down = shifted(pk_hi, "grp", 1)
     far = [shifted(lists, "grp", d) for d in range(2, strips - 1)]
 
-    force_shape = shape((3 * places * 8, 128), f32)
+    force_shape = shape((3 * (places + 1) * 8, 128), f32)
+    pairs = [vm((24 * (places + 1), 128), f32)] + [vm((128, 512), f32)] * UNROLL
+
+    def sources(blocks):
+        return vm((blocks * places * 8, 128), f32)
+
     table_shape = (2, XW * YR, terms * 256)
     line, edge_table, partial, force = call(
         tables_kernel,
@@ -585,8 +673,8 @@
             vm((8, 128), f32),
             vm(table_shape, bf16),
             vm((2, terms * 256, depth), bf16),
-            vm((1, 128, 128), f32),
-            vm(force_shape.shape, f32),
+            sources(1),
+            *pairs,
         ],
         kernel_taps, own, pos,
         flops=10**10, name="tables",
@@ -606,11 +694,11 @@
     e_hi = shifted(edge_low, "patch", -2)
     e_lo = shifted(edge_high, "patch", 2)
 
-    work = shape((4 * strips * slots + 8,), i32)
+    work = shape((4 * strips * slots + 16,), i32)
     force, work_near, work_far = call(
         functools.partial(near_kernel, number_far=number_far, strips=strips),
         [force_shape, work, work],
-        [pltpu.SMEM((strips, 8, 128), f32), vm((3, 128, 128), f32), pltpu.SemaphoreType.DMA((strips,))],
+        [pltpu.SMEM((strips, 8, 128), f32), sources(3), *pairs, pltpu.SemaphoreType.DMA((strips,))],
         up, down, pos, lists, *far, force,
         flops=10**10, smem_out=(1, 2), name="near",
     )
@@ -621,11 +709,12 @@
         [
             vm(force_shape.shape, f32),
             pltpu.SMEM((strips, 8, 128), f32),
-            vm((6, 128, 128), f32),
+            sources(6),
             vm((XO * YR, depth), f32),
             vm((depth + 2 * PZ, XO * YR), f32),
             vm((3, places, atoms), f32),
             pltpu.SemaphoreType.DMA((strips,)),
+            *pairs,
         ],
         cells, offsets, charges, masses, velocity, pos, mid, low, high, e_lo, e_hi, force, work_far,
         smem=(12,), smem_out=(2,), name="sample",
@@ -636,7 +725,7 @@
     force = call(
         moved_self_kernel,
         [force_shape],
-        [vm((rows, 128), f32), vm((1, 128, 128), f32)],
+        [sources(1), *pairs],
         moved, pos,
         flops=10**10, name="moved_self",
     )[0]
@@ -646,14 +735,14 @@
     force = call(
         moved_near_kernel,
         [force_shape],
-        [vm((rows, 128), f32), vm((3, 128, 128), f32)],
+        [sources(3), *pairs],
         moved, moved_up, moved_down, pos, up, down, force, work_near,
         smem=(7,), flops=10**10, name="moved_near",
     )[0]
     shown, speed = call(
         moved_far_kernel,
         [shape((3, places, atoms), f32)] * 2,
-        [vm(force_shape.shape, f32), vm((rows, 128), f32), vm((6, 128, 128), f32)],
+        [vm(force_shape.shape, f32), sources(6), *pairs],
         moved, moved_low, moved_high, pos, low, high, force, work_far, work_below, half, masses,
         smem=(7, 8), name="moved_far",
     )

time: 90.9 us -> 66.2 us (0.73)
  Pallas kernels: 70.9 us -> 34.5 us
  waiting for transfers between devices: 1.34 us -> 8.75 us
  local copies, waits for them, and re-layouts: 2.24 us -> 4.34 us
  starting transfers between devices: 14.1 us -> 15.9 us
    pallas_call x8, Pallas kernels: 70.9 us -> 34.5 us  [call(): pl.pallas_call(kernel, out_shape=outs, in_specs=[scalar if n in smem else...]
    ppermute x11, waiting for transfers between devices: 1.34 us -> 8.75 us  [shifted(): lax.ppermute(x, axis, [(i, (i + distance) % size) for i in range(size)])]
    unnamed x26 -> x24, local copies, waits for them, and re-layouts: 2.23 us -> 4.34 us
    ppermute x11, starting transfers between devices: 14.1 us -> 15.9 us  [shifted(): lax.ppermute(x, axis, [(i, (i + distance) % size) for i in range(size)])]
  transfers between devices with their start and end apart: 11 -> 11, of which waited for: 2 -> 5; matrix products, arithmetic and copies ran while one was open for 0% -> 0% of each run, Pallas kernels for 43% -> 27%
where the time goes in v1:
time: 66.2 us; the launch traced here: 64.9 us
  Pallas kernels  34.5 us (52%)
  starting transfers between devices  15.9 us (24%)
  waiting for transfers between devices  8.75 us (13%)
  local copies, waits for them, and re-layouts  4.34 us (7%)
  between operations  1.42 us (2%)
    pallas_call x8, Pallas kernels, call(): pl.pallas_call(kernel, out_shape=outs, in_specs=[scalar if n in smem else...  34.5 us
    ppermute x11, starting transfers between devices, shifted(): lax.ppermute(x, axis, [(i, (i + distance) % size) for i in range(size)])  15.9 us
    ppermute x11, waiting for transfers between devices, shifted(): lax.ppermute(x, axis, [(i, (i + distance) % size) for i in range(size)])  8.75 us
    unnamed x24, local copies, waits for them, and re-layouts  4.34 us
  transfers between devices with their start and end apart: 11, of which 5 were waited for; matrix products, arithmetic and copies ran while one was open for 0% of the time, Pallas kernels for 27%

profile of v1, /device:TPU:3, one launch (start us, length us, event | category | flops | bytes accessed | tf_op | source)
XLA Modules:
  0.0 64.9 jit_solution(1613739545101406699)
XLA Ops:
  1.3 0.0 copy-start
  1.3 0.8 %copy-done = s32[3,1,1,32,128]{4,3,2,1,0:T(8,128)S(1)} copy-done((s32[3,1,1,32,128]{4,3,2,1,0:T(8,128)S(1)}, s32[3,1,1,32,128]{4,3,2,1,0:T(8,128)}, u32[]{:S(2)}) %copy-start) | copy-done | bytes 49176
  2.1 0.0 copy-start.2
  2.1 0.8 %copy-done.2 = f32[3,1,1,32,128]{4,3,2,1,0:T(8,128)S(1)} copy-done((f32[3,1,1,32,128]{4,3,2,1,0:T(8,128)S(1)}, f32[3,1,1,32,128]{4,3,2,1,0:T(8,128)}, u32[]{:S(2)}) %copy-start.2) | copy-done | bytes 49176
  2.9 0.0 copy-start.5
  2.9 0.7 %copy-done.5 = f32[1,1,32,128]{3,2,1,0:T(8,128)S(1)} copy-done((f32[1,1,32,128]{3,2,1,0:T(8,128)S(1)}, f32[1,1,32,128]{3,2,1,0:T(8,128)}, u32[]{:S(2)}) %copy-start.5) | copy-done | bytes 16408
  3.6 0.0 copy-start.8
  3.6 0.7 %copy-done.8 = s32[1,1,32]{2,1,0:T(1,128)S(1)} copy-done((s32[1,1,32]{2,1,0:T(1,128)S(1)}, s32[1,1,32]{2,1,0:T(1,128)}, u32[]{:S(2)}) %copy-start.8) | copy-done | bytes 152
  4.3 0.0 copy-start.9
  4.3 0.7 %copy-done.9 = s32[1,1,32]{2,1,0:T(1,128)S(1)} copy-done((s32[1,1,32]{2,1,0:T(1,128)S(1)}, s32[1,1,32]{2,1,0:T(1,128)}, u32[]{:S(2)}) %copy-start.9) | copy-done | bytes 152
  4.9 2.1 %spread.1 = (f32[240,256]{1,0:T(8,128)S(1)}, f32[344,128]{1,0:T(8,128)S(1)}, f32[344,128]{1,0:T(8,128)S(1)}, f32[128,128]{1,0:T(8,128)S(1)}, f32[8,128]{1,0:T(8,128)S(1)}) custom-call(s32[3,32,128]{2,1,0:T(8,128)S(1)} %bitcast.13, f32[3,32,128]{2,1,0:T(8,128)S(1)} %bitcast.15, f32[32,128]{1,0:T(8,128)S(1)} %bitcast.19, s32[1,32]{1,0:T(1,128)S(1)} %bitcast.22, ...), custom_call_target="tpu_custom_call" | custom-call | bytes 1048576 | tf_op jit(solution)/shard_map/spread/pallas_call | solution.py:613
  7.0 2.4 %collective-permute-start.2 = (f32[8,128]{1,0:T(8,128)S(1)}, f32[8,128]{1,0:T(8,128)S(1)}, u32[]{:S(2)}, u32[]{:S(2)}) collective-permute-start(f32[8,128]{1,0:T(8,128)S(1)} %get-tuple-element.27.refs_3_), channel_id=1, source_target_pairs={{0,2},{1,3},{2,0},{3,1},{4,6},{5,7},{6,4},{7,5},{8,10},{9,11},{10,... | collective-permute-start | bytes 12296 | tf_op jit(solution)/shard_map/ppermute | solution.py:627
  9.4 1.1 %collective-permute-start = (f32[344,128]{1,0:T(8,128)S(1)}, f32[344,128]{1,0:T(8,128)S(1)}, u32[]{:S(2)}, u32[]{:S(2)}) collective-permute-start(f32[344,128]{1,0:T(8,128)S(1)} %get-tuple-element.25), channel_id=1, source_target_pairs={{0,3},{1,0},{2,1},{3,2},{4,7},{5,4},{6,5},{7,6},{8,11},{9,8},{10,9... | collective-permute-start | bytes 528392 | tf_op jit(solution)/shard_map/ppermute | solution.py:627
  10.5 0.4 collective-permute-start.1
  10.9 0.7 %copy-done.10 = f32[6,17]{1,0:T(8,128)S(1)} copy-done((f32[6,17]{1,0:T(8,128)S(1)}, f32[6,17]{1,0:T(8,128)}, u32[]{:S(2)}) %copy-start.10) | copy-done | bytes 432
  11.6 6.4 %tables.1 = (bf16[2,6,256,256]{3,2,1,0:T(8,128)(2,1)S(1)}, bf16[2,624,1536]{2,1,0:T(8,128)(2,1)S(1)}, f32[624,256]{1,0:T(8,128)S(1)}, f32[792,128]{1,0:T(8,128)S(1)}) custom-call(f32[6,17]{1,0:T(8,128)S(1)} %copy-done.10, f32[240,256]{1,0:T(8,128)S(1)} %get-tuple-element.28.own, f32[128,128]{1,0:T(8,128)S(1)} %get-tuple-element.24.pos.refs_2_), custom_call_target="tpu_custom_call" | custom-call | flops 10000000000 | bytes 1048576 | tf_op jit(solution)/shard_map/tables/pallas_call | solution.py:613
  18.0 0.0 collective-permute-done.2.refs_4_
  18.0 0.0 collective-permute-done.refs_0_.up_pk
  18.0 0.6 collective-permute-done.1.refs_1_.down_pk
  18.6 2.3 %planes.1 = (f32[784,128]{1,0:T(8,128)S(1)}, f32[784,128]{1,0:T(8,128)S(1)}, f32[80,128]{1,0:T(8,128)S(1)}, f32[80,128]{1,0:T(8,128)S(1)}, f32[240,256]{1,0:T(8,128)S(1)}) custom-call(f32[344,128]{1,0:T(8,128)S(1)} %collective-permute-done.refs_0_.up_pk, f32[344,128]{1,0:T(8,128)S(1)} %collective-permute-done.1.refs_1_.down_pk, ...), custom_call_target="tpu_custom_call" | custom-call | bytes 1048576 | tf_op jit(solution)/shard_map/planes/pallas_call | solution.py:613
  20.9 1.3 %collective-permute-start.5 = (f32[80,128]{1,0:T(8,128)S(1)}, f32[80,128]{1,0:T(8,128)S(1)}, u32[]{:S(2)}, u32[]{:S(2)}) collective-permute-start(f32[80,128]{1,0:T(8,128)S(1)} %get-tuple-element.35), channel_id=1, source_target_pairs={{0,8},{4,12},{8,16},{12,20},{16,24},{20,28},{24,0},{28,4},{1,9},{5... | collective-permute-start | bytes 122888 | tf_op jit(solution)/shard_map/ppermute | solution.py:627
  22.1 0.3 collective-permute-start.6
  22.4 4.0 %collective-permute-start.3 = (f32[784,128]{1,0:T(8,128)S(1)}, f32[784,128]{1,0:T(8,128)S(1)}, u32[]{:S(2)}, u32[]{:S(2)}) collective-permute-start(f32[784,128]{1,0:T(8,128)S(1)} %get-tuple-element.33), channel_id=1, source_target_pairs={{0,4},{4,8},{8,12},{12,16},{16,20},{20,24},{24,28},{28,0},{1,5},{5... | collective-permute-start | bytes 1204232 | tf_op jit(solution)/shard_map/ppermute | solution.py:627
  26.4 0.0 collective-permute-start.4
  26.5 0.0 copy-start.6
  26.5 0.0 copy-start.7
  26.5 5.4 %near.1 = (f32[792,128]{1,0:T(8,128)S(1)}, s32[528]{0:T(1024)S(1)}, s32[528]{0:T(1024)S(1)}) custom-call(f32[344,128]{1,0:T(8,128)S(1)} %collective-permute-done.refs_0_.up_pk, f32[344,128]{1,0:T(8,128)S(1)} %collective-permute-done.1.refs_1_.down_pk, f32[128,128]{1,0:T(8,128)S(1)} %get-tuple-element.24.pos.refs_2_, f32[8,128]{1,0:T(8,128)S(1)} %get-tuple-element.27.refs_3_, ...), custom_call_target="tpu_custom_call" | custom-call | flops 10000000000 | bytes 1048576 | tf_op jit(solution)/shard_map/near/pallas_call | solution.py:613
  31.9 0.0 collective-permute-done.5.e_lo
  31.9 0.0 collective-permute-done.6.e_hi
  31.9 3.6 %collective-permute-done.3.low.low_pk = f32[784,128]{1,0:T(8,128)S(1)} collective-permute-done((f32[784,128]{1,0:T(8,128)S(1)}, f32[784,128]{1,0:T(8,128)S(1)}, u32[]{:S(2)}, u32[]{:S(2)}) %collective-permute-start.3) | collective-permute-done | bytes 401440 | tf_op jit(solution)/shard_map/ppermute | solution.py:627
  35.5 1.2 %collective-permute-done.4.high.high_pk = f32[784,128]{1,0:T(8,128)S(1)} collective-permute-done((f32[784,128]{1,0:T(8,128)S(1)}, f32[784,128]{1,0:T(8,128)S(1)}, u32[]{:S(2)}, u32[]{:S(2)}) %collective-permute-start.4) | collective-permute-done | bytes 401440 | tf_op jit(solution)/shard_map/ppermute | solution.py:627
  36.7 0.0 copy-done.1
  36.7 0.0 copy-done.3
  36.7 0.0 copy-done.4
  36.7 0.0 copy-done.6
  36.7 0.0 copy-done.7
  36.8 8.0 %sample.1 = (f32[3,32,128]{2,1,0:T(8,128)S(1)}, f32[96,128]{1,0:T(8,128)S(1)}, s32[528]{0:T(1024)S(1)}) custom-call(s32[3,32,128]{2,1,0:T(8,128)S(1)} %bitcast.14, f32[3,32,128]{2,1,0:T(8,128)S(1)} %bitcast.16, f32[32,128]{1,0:T(8,128)S(1)} %bitcast.20, f32[32,128]{1,0:T(8,128)S(1)} %bitcast.17, f32[3,32,128]{2,1,0:T(8,128)S(1)} %bitcast.21, ...), custom_call_target="tpu_custom_call" | custom-call | bytes 1048576 | tf_op jit(solution)/shard_map/sample/pallas_call | solution.py:613
  44.7 2.4 %collective-permute-start.8 = (f32[96,128]{1,0:T(8,128)S(1)}, f32[96,128]{1,0:T(8,128)S(1)}, u32[]{:S(2)}, u32[]{:S(2)}) collective-permute-start(f32[96,128]{1,0:T(8,128)S(1)} %get-tuple-element.40.moved), channel_id=1, source_target_pairs={{0,3},{1,0},{2,1},{3,2},{4,7},{5,4},{6,5},{7,6},{8,11},{9,8},{10,9... | collective-permute-start | bytes 147464 | tf_op jit(solution)/shard_map/ppermute | solution.py:627
  47.1 0.0 collective-permute-start.7
  47.1 3.3 %moved_self.1.force_in = f32[792,128]{1,0:T(8,128)S(1)} custom-call(f32[96,128]{1,0:T(8,128)S(1)} %get-tuple-element.40.moved, f32[128,128]{1,0:T(8,128)S(1)} %get-tuple-element.24.pos.refs_2_), custom_call_target="tpu_custom_call" | custom-call | flops 10000000000 | bytes 1048576 | tf_op jit(solution)/shard_map/moved_self/pallas_call | solution.py:613
  50.4 1.7 %collective-permute-done.7.down = f32[96,128]{1,0:T(8,128)S(1)} collective-permute-done((f32[96,128]{1,0:T(8,128)S(1)}, f32[96,128]{1,0:T(8,128)S(1)}, u32[]{:S(2)}, u32[]{:S(2)}) %collective-permute-start.7) | collective-permute-done | bytes 49184 | tf_op jit(solution)/shard_map/ppermute | solution.py:627
  52.2 0.0 collective-permute-done.8.up
  52.2 1.0 %collective-permute-start.10 = (f32[288,128]{1,0:T(8,128)S(1)}, f32[288,128]{1,0:T(8,128)S(1)}, u32[]{:S(2)}, u32[]{:S(2)}) collective-permute-start(f32[288,128]{1,0:T(8,128)S(1)} %constant_dynamic-update-slice_fusion), channel_id=1, source_target_pairs={{0,28},{4,0},{8,4},{12,8},{16,12},{20,16},{24,20},{28,24},{1,29},{... | collective-permute-start | bytes 442376 | tf_op jit(solution)/shard_map/ppermute | solution.py:627
  53.1 3.2 %collective-permute-start.9 = (f32[288,128]{1,0:T(8,128)S(1)}, f32[288,128]{1,0:T(8,128)S(1)}, u32[]{:S(2)}, u32[]{:S(2)}) collective-permute-start(f32[288,128]{1,0:T(8,128)S(1)} %constant_dynamic-update-slice_fusion), channel_id=1, source_target_pairs={{0,4},{4,8},{8,12},{12,16},{16,20},{20,24},{24,28},{28,0},{1,5},{5... | collective-permute-start | bytes 442376 | tf_op jit(solution)/shard_map/ppermute | solution.py:627
  56.3 2.5 %moved_near.1.force_in = f32[792,128]{1,0:T(8,128)S(1)} custom-call(f32[96,128]{1,0:T(8,128)S(1)} %get-tuple-element.40.moved, f32[96,128]{1,0:T(8,128)S(1)} %collective-permute-done.8.up, f32[96,128]{1,0:T(8,128)S(1)} %collective-permute-done.7.down, f32[128,128]{1,0:T(8,128)S(1)} %get-tuple-element.24.pos.refs_2_, ...), custom_call_target="tpu_custom_call" | custom-call | flops 10000000000 | bytes 1048576 | tf_op jit(solution)/shard_map/moved_near/pallas_call | solution.py:613
  58.8 1.6 %collective-permute-done.10.high = f32[288,128]{1,0:T(8,128)S(1)} collective-permute-done((f32[288,128]{1,0:T(8,128)S(1)}, f32[288,128]{1,0:T(8,128)S(1)}, u32[]{:S(2)}, u32[]{:S(2)}) %collective-permute-start.10) | collective-permute-done | bytes 147488 | tf_op jit(solution)/shard_map/ppermute | solution.py:627
  60.5 0.0 collective-permute-done.9.low
  60.5 4.4 %moved_far.1 = (f32[3,32,128]{2,1,0:T(8,128)}, f32[3,32,128]{2,1,0:T(8,128)}) custom-call(f32[96,128]{1,0:T(8,128)S(1)} %get-tuple-element.40.moved, f32[288,128]{1,0:T(8,128)S(1)} %collective-permute-done.9.low, f32[288,128]{1,0:T(8,128)S(1)} %collective-permute-done.10.high, f32[128,128]{1,0:T(8,128)S(1)} %get-tuple-element.24.pos.refs_2_, ...), custom_call_target="tpu_custom_call" | custom-call | bytes 1048576 | tf_op jit(solution)/shard_map/moved_far/pallas_call | solution.py:613
  (7 shorter events, 0.0 us)
Async XLA Ops:
  1.3 0.8 %copy-start = (s32[3,1,1,32,128]{4,3,2,1,0:T(8,128)S(1)}, s32[3,1,1,32,128]{4,3,2,1,0:T(8,128)}, u32[]{:S(2)}) copy-start(s32[3,1,1,32,128]{4,3,2,1,0:T(8,128)} %param.9) | copy-start | bytes 147460
  2.1 0.8 %copy-start.2 = (f32[3,1,1,32,128]{4,3,2,1,0:T(8,128)S(1)}, f32[3,1,1,32,128]{4,3,2,1,0:T(8,128)}, u32[]{:S(2)}) copy-start(f32[3,1,1,32,128]{4,3,2,1,0:T(8,128)} %param.10) | copy-start | bytes 147460
  2.9 0.7 %copy-start.5 = (f32[1,1,32,128]{3,2,1,0:T(8,128)S(1)}, f32[1,1,32,128]{3,2,1,0:T(8,128)}, u32[]{:S(2)}) copy-start(f32[1,1,32,128]{3,2,1,0:T(8,128)} %param.11) | copy-start | bytes 49156
  3.6 0.7 %copy-start.8 = (s32[1,1,32]{2,1,0:T(1,128)S(1)}, s32[1,1,32]{2,1,0:T(1,128)}, u32[]{:S(2)}) copy-start(s32[1,1,32]{2,1,0:T(1,128)} %param.14) | copy-start | bytes 388
  4.3 0.7 %copy-start.9 = (s32[1,1,32]{2,1,0:T(1,128)S(1)}, s32[1,1,32]{2,1,0:T(1,128)}, u32[]{:S(2)}) copy-start(s32[1,1,32]{2,1,0:T(1,128)} %param.15) | copy-start | bytes 388
  7.0 10.9 %collective-permute-start.2 = (f32[8,128]{1,0:T(8,128)S(1)}, f32[8,128]{1,0:T(8,128)S(1)}, u32[]{:S(2)}, u32[]{:S(2)}) collective-permute-start(f32[8,128]{1,0:T(8,128)S(1)} %get-tuple-element.27.refs_3_), channel_id=1, source_target_pairs={{0,2},{1,3},{2,0},{3,1},{4,6},{5,7},{6,4},{7,5},{8,10},{9,11},{10,... | collective-permute-start | bytes 12296 | tf_op jit(solution)/shard_map/ppermute | solution.py:627
  9.4 8.6 %collective-permute-start = (f32[344,128]{1,0:T(8,128)S(1)}, f32[344,128]{1,0:T(8,128)S(1)}, u32[]{:S(2)}, u32[]{:S(2)}) collective-permute-start(f32[344,128]{1,0:T(8,128)S(1)} %get-tuple-element.25), channel_id=1, source_target_pairs={{0,3},{1,0},{2,1},{3,2},{4,7},{5,4},{6,5},{7,6},{8,11},{9,8},{10,9... | collective-permute-start | bytes 528392 | tf_op jit(solution)/shard_map/ppermute | solution.py:627
  10.5 8.1 %collective-permute-start.1 = (f32[344,128]{1,0:T(8,128)S(1)}, f32[344,128]{1,0:T(8,128)S(1)}, u32[]{:S(2)}, u32[]{:S(2)}) collective-permute-start(f32[344,128]{1,0:T(8,128)S(1)} %get-tuple-element.26), channel_id=1, source_target_pairs={{0,1},{1,2},{2,3},{3,0},{4,5},{5,6},{6,7},{7,4},{8,9},{9,10},{10,1... | collective-permute-start | bytes 528392 | tf_op jit(solution)/shard_map/ppermute | solution.py:627
  10.9 0.7 %copy-start.10 = (f32[6,17]{1,0:T(8,128)S(1)}, f32[6,17]{1,0:T(8,128)}, u32[]{:S(2)}) copy-start(f32[6,17]{1,0:T(8,128)} %taps_in.1) | copy-start | bytes 1228
  20.9 11.1 %collective-permute-start.5 = (f32[80,128]{1,0:T(8,128)S(1)}, f32[80,128]{1,0:T(8,128)S(1)}, u32[]{:S(2)}, u32[]{:S(2)}) collective-permute-start(f32[80,128]{1,0:T(8,128)S(1)} %get-tuple-element.35), channel_id=1, source_target_pairs={{0,8},{4,12},{8,16},{12,20},{16,24},{20,28},{24,0},{28,4},{1,9},{5... | collective-permute-start | bytes 122888 | tf_op jit(solution)/shard_map/ppermute | solution.py:627
  22.1 9.8 %collective-permute-start.6 = (f32[80,128]{1,0:T(8,128)S(1)}, f32[80,128]{1,0:T(8,128)S(1)}, u32[]{:S(2)}, u32[]{:S(2)}) collective-permute-start(f32[80,128]{1,0:T(8,128)S(1)} %get-tuple-element.36), channel_id=1, source_target_pairs={{0,24},{4,28},{8,0},{12,4},{16,8},{20,12},{24,16},{28,20},{1,25},{... | collective-permute-start | bytes 122888 | tf_op jit(solution)/shard_map/ppermute | solution.py:627
  22.4 13.2 %collective-permute-start.3 = (f32[784,128]{1,0:T(8,128)S(1)}, f32[784,128]{1,0:T(8,128)S(1)}, u32[]{:S(2)}, u32[]{:S(2)}) collective-permute-start(f32[784,128]{1,0:T(8,128)S(1)} %get-tuple-element.33), channel_id=1, source_target_pairs={{0,4},{4,8},{8,12},{12,16},{16,20},{20,24},{24,28},{28,0},{1,5},{5... | collective-permute-start | bytes 1204232 | tf_op jit(solution)/shard_map/ppermute | solution.py:627
  26.4 10.3 %collective-permute-start.4 = (f32[784,128]{1,0:T(8,128)S(1)}, f32[784,128]{1,0:T(8,128)S(1)}, u32[]{:S(2)}, u32[]{:S(2)}) collective-permute-start(f32[784,128]{1,0:T(8,128)S(1)} %get-tuple-element.34), channel_id=1, source_target_pairs={{0,28},{4,0},{8,4},{12,8},{16,12},{20,16},{24,20},{28,24},{1,29},{... | collective-permute-start | bytes 1204232 | tf_op jit(solution)/shard_map/ppermute | solution.py:627
  26.4 10.3 %copy-start.1 = (s32[3,1,1,32,128]{4,3,2,1,0:T(8,128)S(1)}, s32[3,1,1,32,128]{4,3,2,1,0:T(8,128)}, u32[]{:S(2)}) copy-start(s32[3,1,1,32,128]{4,3,2,1,0:T(8,128)} %param.9) | copy-start | bytes 147460
  26.4 10.3 %copy-start.3 = (f32[3,1,1,32,128]{4,3,2,1,0:T(8,128)S(1)}, f32[3,1,1,32,128]{4,3,2,1,0:T(8,128)}, u32[]{:S(2)}) copy-start(f32[3,1,1,32,128]{4,3,2,1,0:T(8,128)} %param.10) | copy-start | bytes 147460
  26.4 10.3 %copy-start.4 = (f32[1,1,32,128]{3,2,1,0:T(8,128)S(1)}, f32[1,1,32,128]{3,2,1,0:T(8,128)}, u32[]{:S(2)}) copy-start(f32[1,1,32,128]{3,2,1,0:T(8,128)} %param.12) | copy-start | bytes 49156
  26.5 10.3 %copy-start.6 = (f32[1,1,32,128]{3,2,1,0:T(8,128)S(1)}, f32[1,1,32,128]{3,2,1,0:T(8,128)}, u32[]{:S(2)}) copy-start(f32[1,1,32,128]{3,2,1,0:T(8,128)} %param.11) | copy-start | bytes 49156
  26.5 10.3 %copy-start.7 = (f32[3,1,1,32,128]{4,3,2,1,0:T(8,128)S(1)}, f32[3,1,1,32,128]{4,3,2,1,0:T(8,128)}, u32[]{:S(2)}) copy-start(f32[3,1,1,32,128]{4,3,2,1,0:T(8,128)} %param.13) | copy-start | bytes 147460
  44.7 7.4 %collective-permute-start.8 = (f32[96,128]{1,0:T(8,128)S(1)}, f32[96,128]{1,0:T(8,128)S(1)}, u32[]{:S(2)}, u32[]{:S(2)}) collective-permute-start(f32[96,128]{1,0:T(8,128)S(1)} %get-tuple-element.40.moved), channel_id=1, source_target_pairs={{0,3},{1,0},{2,1},{3,2},{4,7},{5,4},{6,5},{7,6},{8,11},{9,8},{10,9... | collective-permute-start | bytes 147464 | tf_op jit(solution)/shard_map/ppermute | solution.py:627
  47.1 5.1 %collective-permute-start.7 = (f32[96,128]{1,0:T(8,128)S(1)}, f32[96,128]{1,0:T(8,128)S(1)}, u32[]{:S(2)}, u32[]{:S(2)}) collective-permute-start(f32[96,128]{1,0:T(8,128)S(1)} %get-tuple-element.40.moved), channel_id=1, source_target_pairs={{0,1},{1,2},{2,3},{3,0},{4,5},{5,6},{6,7},{7,4},{8,9},{9,10},{10,1... | collective-permute-start | bytes 147464 | tf_op jit(solution)/shard_map/ppermute | solution.py:627
  52.2 8.3 %collective-permute-start.10 = (f32[288,128]{1,0:T(8,128)S(1)}, f32[288,128]{1,0:T(8,128)S(1)}, u32[]{:S(2)}, u32[]{:S(2)}) collective-permute-start(f32[288,128]{1,0:T(8,128)S(1)} %constant_dynamic-update-slice_fusion), channel_id=1, source_target_pairs={{0,28},{4,0},{8,4},{12,8},{16,12},{20,16},{24,20},{28,24},{1,29},{... | collective-permute-start | bytes 442376 | tf_op jit(solution)/shard_map/ppermute | solution.py:627
  53.1 7.3 %collective-permute-start.9 = (f32[288,128]{1,0:T(8,128)S(1)}, f32[288,128]{1,0:T(8,128)S(1)}, u32[]{:S(2)}, u32[]{:S(2)}) collective-permute-start(f32[288,128]{1,0:T(8,128)S(1)} %constant_dynamic-update-slice_fusion), channel_id=1, source_target_pairs={{0,4},{4,8},{8,12},{12,16},{16,20},{20,24},{24,28},{28,0},{1,5},{5... | collective-permute-start | bytes 442376 | tf_op jit(solution)/shard_map/ppermute | solution.py:627
